TPU v7x, 32 devices: a whole 2x2x4 slice. The times are simulated.
32 devices in a mesh: row: 4 (over x, core), col: 8 (over z, y).
Axes of the slice: x: 2, y: 2, z: 4, core: 2. Of those that a mesh axis runs over, the one named last changes fastest.
Arguments:
- centres: float32 [65536, 64], P(('row', 'col')), may hold values from -6 to 6
- weights: float32 [65536, 64], P(('row', 'col')), may hold values from -0.25 to 0.25
- targets: float32 [512, 64], replicated, may hold values from -6 to 6
- batch_index: int32 [512], replicated, may hold values from 0 to 65535
- nystrom_index: int32 [4096], replicated, may hold values from 0 to 65535
- eigvecs: float32 [4096, 1024], P('row', 'col'), may hold values from -0.09375 to 0.09375
- mode_scale: float32 [1024], P('col'), may hold values from 0.02 to 0.2
Outputs:
- residual: float32 [512, 64], replicated
- step: float32 [65536, 64], P(('row', 'col'))
All inputs are finite; a program needn't handle non-finite values.
Results may differ from a plain program's by a relative error of at most 0.0001.
Values sent between devices are 32-bit elements; how exact they have to be, the bound alone decides.
A program may use at most 128 MiB of HBM per device.

v0:
```python
import jax
import jax.numpy as jnp
from jax import lax
from jax.sharding import PartitionSpec as P

learning_rate = 0.25


def kernel(left, right):
    left_sq = jnp.sum(left * left, axis=1)
    right_sq = jnp.sum(right * right, axis=1)
    inner_prod = jnp.dot(
        left, right.T, precision=lax.Precision.HIGHEST, preferred_element_type=jnp.float32
    )
    return jnp.exp(
        -(left_sq[:, None] + right_sq[None, :] - 2.0 * inner_prod) / float(left.shape[1])
    )


def product(left, right):
    return jnp.dot(left, right, precision=lax.Precision.HIGHEST, preferred_element_type=jnp.float32)


def local(centres, weights, targets, batch_index, nystrom_index, eigvecs, mode_scale):
    rows_dev = centres.shape[0]
    block_rows = eigvecs.shape[0]
    offset = lax.axis_index(("row", "col")) * rows_dev

    def select_rows(index):
        local_rows = index - offset
        inside = (local_rows >= 0) & (local_rows < rows_dev)
        fetched = jnp.take(centres, jnp.clip(local_rows, 0, rows_dev - 1), axis=0)
        return jnp.where(inside[:, None], fetched, 0.0)

    batch_feats, nystrom = lax.psum(
        (select_rows(batch_index), select_rows(nystrom_index)), ("row", "col")
    )
    nys_block = lax.dynamic_slice_in_dim(nystrom, lax.axis_index("row") * block_rows, block_rows, 0)
    kern_batch = kernel(centres, batch_feats)
    partial_pred = lax.dot_general(
        kern_batch,
        weights,
        (((0,), (0,)), ((), ())),
        precision=lax.Precision.HIGHEST,
        preferred_element_type=jnp.float32,
    )
    prediction = lax.psum(partial_pred, ("row", "col"))
    residual = prediction - targets
    gradient = product(kernel(nys_block, batch_feats), residual)
    mode_terms = lax.dot_general(
        eigvecs,
        gradient,
        (((0,), (0,)), ((), ())),
        precision=lax.Precision.HIGHEST,
        preferred_element_type=jnp.float32,
    )
    coeff = mode_scale[:, None] * lax.psum(mode_terms, "row")
    correction = lax.psum(product(eigvecs, coeff), "col")
    direct = product(kern_batch, residual)
    folded = direct - product(
        kernel(centres, nystrom), lax.all_gather(correction, "row", axis=0, tiled=True)
    )
    step = learning_rate * folded
    return (residual, step)


def solution(mesh):
    in_specs = (
        P(("row", "col"), None),
        P(("row", "col"), None),
        P(),
        P(),
        P(),
        P("row", "col"),
        P("col"),
    )
    out_specs = (P(), P(("row", "col"), None))
    return jax.shard_map(local, mesh=mesh, in_specs=in_specs, out_specs=out_specs, check_vma=False)
```

profile of v0, /device:TPU:0, one launch (start us, length us, event | category | flops | bytes accessed | tf_op | source)
XLA Modules:
  0.0 467.1 jit_solution(167002956576013100)
XLA Ops:
  7.2 0.0 copy-start
  7.2 0.0 all-reduce.5.cloned.1.call-start
  7.2 0.7 compare_and_fusion.2
  8.0 0.0 copy-start.8
  8.0 1.4 copy.9
  9.4 1.0 gather_fusion
  10.4 0.9 select_select_fusion.1
  11.3 0.0 all-reduce.5.cloned.1.call-update
  11.4 0.0 all-reduce.9.cloned.1.call-start
  11.4 0.0 copy-done.8
  11.5 14.2 %gather_fusion.1 = f32[4096,64]{1,0:T(8,128)} fusion(f32[2048,64]{1,0:T(8,128)S(1)} %copy.9, s32[4096]{0:T(1024)S(1)} %fusion.30), kind=kCustom, calls=%fused_computation.1 | custom fusion | bytes 2113536 | tf_op jit(solution)/shard_map/jit(_take)/gather | solution.py:32
  25.7 6.0 %select_select_fusion = f32[4096,64]{1,0:T(8,128)} fusion(f32[4096,64]{1,0:T(8,128)} %gather_fusion.1, pred[4096]{0:T(1024)(128)(4,1)S(1)} %get-tuple-element.7, pred[4096]{0:T(1024)(128)(4,1)S(1)} %get-tuple-element.6), kind=kLoop, calls=%fused_computation.27 | loop fusion | flops 524288 | bytes 2105344 | tf_op jit(solution)/shard_map/jit(_where)/select_n | solution.py:33
  31.7 0.0 copy-done.3
  31.7 0.1 multiply_reduce_fusion.2
  31.8 111.6 %all-reduce.5.cloned.1.call-done = f32[512,64]{1,0:T(8,128)} async-done(((f32[512,64]{1,0:T(8,128)}), f32[512,64]{1,0:T(8,128)}) %all-reduce.5.cloned.1.call-update) | async-done | bytes 131088 | tf_op jit(solution)/shard_map/psum | solution.py:35
  143.3 1.1 multiply_reduce_fusion.3
  144.4 0.0 copy-start.5
  144.4 5.1 %fusion.13 = f32[2048,512]{0,1:T(8,128)S(1)} fusion(f32[512,64]{1,0:T(8,128)} %all-reduce.5.cloned.1.call-done, f32[2048,64]{0,1:T(8,128)S(1)} %copy-done.3, f32[512]{0:T(512)S(1)} %multiply_reduce_fusion.3, f32[2048]{0:T(1024)S(1)} %multiply_reduce_fusion.2), kind=kOutput, calls=%fused_computation.16 | convolution fusion | flops 810549248 | bytes 4859904 | tf_op jit(solution)/shard_map/dot_general | solution.py:12
  149.5 0.0 copy-start.1
  149.5 2.0 copy-done.1
  151.6 0.0 copy-done.5
  151.6 4.8 %fusion.36 = f32[512,64]{0,1:T(8,128)} fusion(f32[2048,512]{0,1:T(8,128)S(1)} %fusion.13, f32[2048,64]{0,1:T(8,128)S(1)} %copy-done.5), kind=kOutput, calls=%fused_computation.55 | convolution fusion | flops 805306368 | bytes 4849664 | tf_op jit(solution)/shard_map/dot_general | solution.py:40
  156.4 0.0 all-reduce.9.cloned.1.call-update
  156.4 0.2 all-reduce.7.cloned.1.call-start
  156.7 134.4 %all-reduce.9.cloned.1.call-done = (f32[512,64]{0,1:T(8,128)}, f32[4096,64]{1,0:T(8,128)}) async-done(((f32[512,64]{0,1:T(8,128)}, f32[4096,64]{1,0:T(8,128)}), (f32[512,64]{0,1:T(8,128)}, f32[4096,64]{1,0:T(8,128)})) %all-reduce.9.cloned.1.call-update) | async-done | bytes 1179664 | tf_op jit(solution)/shard_map/psum | solution.py:47
  291.1 0.0 copy-done.7
  291.1 0.9 sub.30
  292.0 0.0 copy-start.6
  292.0 1.3 multiply_reduce_fusion.1
  293.3 0.0 copy-done.4
  293.3 2.8 fusion.26
  296.2 0.0 copy-start.9
  296.2 0.0 copy-start.2
  296.2 2.1 fusion.15
  298.3 0.0 copy-done
  298.3 1.0 convolution_bitcast_fusion.1
  299.3 10.7 %psum.38 = f32[128,64]{1,0:T(8,128)S(1)} all-reduce(f32[128,64]{1,0:T(8,128)S(1)} %convolution_bitcast_fusion.1), channel_id=1, replica_groups=mesh['row'=4,'col'=8] {'row'}, use_global_device_ids=true, to_apply=%region_7.8 | all-reduce | flops 8192 | bytes 65536 | tf_op jit(solution)/shard_map/psum | solution.py:57
  310.0 0.0 copy-done.9
  310.0 1.5 convolution_bitcast_fusion
  311.4 0.0 all-reduce.7.cloned.1.call-update
  311.5 0.3 all-gather.2.cloned.1.call-start
  311.7 0.0 copy-done.2
  311.8 0.6 multiply_reduce_fusion
  312.4 69.5 %all-reduce.7.cloned.1.call-done = f32[1024,64]{0,1:T(8,128)} async-done(((f32[1024,64]{0,1:T(8,128)}), f32[1024,64]{0,1:T(8,128)}) %all-reduce.7.cloned.1.call-update) | async-done | bytes 262160 | tf_op jit(solution)/shard_map/psum | solution.py:58
  381.9 0.0 all-gather.2.cloned.1.call-update
  381.9 30.2 %fusion.37 = f32[4096,2048]{0,1:T(8,128)} fusion(f32[4096,64]{1,0:T(8,128)S(1)} %copy-done.2, f32[2048,64]{0,1:T(8,128)S(1)} %copy-done.3), kind=kOutput, calls=%fused_computation.56 | convolution fusion | flops 6442450944 | bytes 35127296 | tf_op jit(solution)/shard_map/dot_general | solution.py:12
  412.1 42.7 %fusion.3 = f32[2048,64]{0,1:T(8,128)S(1)} fusion(f32[4096,64]{0,1:T(8,128)} %all-gather.2.cloned.1.call-done, f32[4096,2048]{0,1:T(8,128)} %fusion.37, f32[4096]{0:T(1024)S(1)} %multiply_reduce_fusion, f32[2048]{0:T(1024)S(1)} %multiply_reduce_fusion.2), kind=kOutput, calls=%fused_computation.6 | convolution fusion | flops 6484393984 | bytes 35151872 | tf_op jit(solution)/shard_map/dot_general | solution.py:21
  454.8 5.8 %fusion.14 = f32[2048,64]{0,1:T(8,128)} fusion(f32[2048,64]{0,1:T(8,128)S(1)} %fusion.3, f32[2048,512]{0,1:T(8,128)} %copy-done.1, f32[512,64]{0,1:T(8,128)S(1)} %sub.30), kind=kOutput, calls=%fused_computation.18 | convolution fusion | flops 805568512 | bytes 5373952 | tf_op jit(solution)/shard_map/dot_general | solution.py:21
  (8 shorter events, 0.0 us)
Async XLA Ops:
  7.2 291.1 %copy-start = (f32[1024,128]{1,0:T(8,128)S(1)}, f32[1024,128]{1,0:T(8,128)}, u32[]{:S(2)}) copy-start(f32[1024,128]{1,0:T(8,128)} %param.12) | copy-start | bytes 1572868
  7.2 136.2 %all-reduce.5.cloned.1.call-start = ((), (), s32[]{:S(2)}) async-start(), calls=%async_computation | async-start | bytes 524288 | tf_op jit(solution)/shard_map/psum | solution.py:35
  8.0 3.4 copy-start.8
  11.4 279.7 %all-reduce.9.cloned.1.call-start = ((), (), s32[]{:S(2)}) async-start(), calls=%async_computation.3 | async-start | bytes 4456448 | tf_op jit(solution)/shard_map/psum | solution.py:47
  25.7 6.0 %copy-start.3 = (f32[2048,64]{0,1:T(8,128)S(1)}, f32[2048,64]{0,1:T(8,128)}, u32[]{:S(2)}) copy-start(f32[2048,64]{0,1:T(8,128)} %param.7) | copy-start | bytes 1572868
  144.4 7.1 %copy-start.5 = (f32[2048,64]{0,1:T(8,128)S(1)}, f32[2048,64]{0,1:T(8,128)}, u32[]{:S(2)}) copy-start(f32[2048,64]{0,1:T(8,128)} %param.8) | copy-start | bytes 1572868
  149.5 2.0 copy-start.1
  156.4 134.7 %copy-start.7 = (f32[512,64]{0,1:T(8,128)S(1)}, f32[512,64]{0,1:T(8,128)}, u32[]{:S(2)}) copy-start(f32[512,64]{0,1:T(8,128)} %param.9) | copy-start | bytes 393220
  156.4 136.9 %copy-start.4 = (f32[512,64]{1,0:T(8,128)S(1)}, f32[512,64]{1,0:T(8,128)}, u32[]{:S(2)}) copy-start(f32[512,64]{1,0:T(8,128)} %all-reduce.5.cloned.1.call-done) | copy-start | bytes 393220
  156.4 225.5 %all-reduce.7.cloned.1.call-start = ((), (), s32[]{:S(2)}) async-start(), calls=%async_computation.1 | async-start | bytes 524288 | tf_op jit(solution)/shard_map/psum | solution.py:58
  292.0 162.8 %copy-start.6 = (f32[512,64]{0,1:T(8,128)}, f32[512,64]{0,1:T(8,128)S(1)}, u32[]{:S(2)}) copy-start(f32[512,64]{0,1:T(8,128)S(1)} %sub.30) | copy-start | bytes 393220
  296.2 13.8 %copy-start.9 = (f32[128]{0:T(128)S(1)}, f32[128]{0:T(128)}, u32[]{:S(2)}) copy-start(f32[128]{0:T(128)} %param.13) | copy-start | bytes 1540
  296.2 15.5 %copy-start.2 = (f32[4096,64]{1,0:T(8,128)S(1)}, f32[4096,64]{1,0:T(8,128)}, u32[]{:S(2)}) copy-start(f32[4096,64]{1,0:T(8,128)} %get-tuple-element.3) | copy-start | bytes 3145732
  311.5 100.6 %all-gather.2.cloned.1.call-start = ((), (), s32[]{:S(2)}) async-start(), calls=%async_computation.2 | async-start | bytes 1310720 | tf_op jit(solution)/shard_map/all_gather | solution.py:61
Sparse Core Ops, SparseCore 0:
  14.1 129.2 all-reduce.4
  156.6 134.4 all-reduce.8
  311.6 70.2 all-reduce.6
  383.3 15.8 all-gather.1
where the time goes:
time: 468 us; the launch traced here: 467 us
  waiting for transfers between devices  316 us (68%)
  matrix products  95.9 us (20%)
  local copies, waits for them, and re-layouts  18.7 us (4%)
  between operations  14 us (3%)
  other arithmetic  11.7 us (2%)
  blocking collectives  10.7 us (2%)
    psum x1, waiting for transfers between devices, local(): prediction = lax.psum(partial_pred, ('row', 'col'))  134 us
    psum x1, waiting for transfers between devices, local(): lax.psum((select_rows(batch_index), select_rows(nystrom_index)), ('row',...  112 us
    psum x1, waiting for transfers between devices, local(): correction = lax.psum(product(eigvecs, coeff), 'col')  69.5 us
    dot_general x4, matrix products, product(): jnp.dot(left, right, precision=lax.Precision.HIGHEST, preferred_element_t...  52 us
    dot_general x3, matrix products, kernel(): jnp.dot(left, right.T, precision=lax.Precision.HIGHEST, preferred_element...  38.1 us
    gather x2, local copies, waits for them, and re-layouts, select_rows(): fetched = jnp.take(centres, jnp.clip(local_rows, 0, rows_dev - 1), axis=0)  15.2 us
    psum x1, blocking collectives, local(): coeff = mode_scale[:, None] * lax.psum(mode_terms, 'row')  10.7 us
  transfers between devices with their start and end apart: 4, of which 3 were waited for; matrix products, arithmetic and copies ran while one was open for 11% of the time, Pallas kernels for 0%

commit v1 on v0

--- a/solution.py
+++ b/solution.py
@@ -44,7 +44,7 @@
         precision=lax.Precision.HIGHEST,
         preferred_element_type=jnp.float32,
     )
-    prediction = lax.psum(partial_pred, ("row", "col"))
+    prediction = jnp.sum(lax.all_gather(partial_pred, ("row", "col")), axis=0)
     residual = prediction - targets
     gradient = product(kernel(nys_block, batch_feats), residual)
     mode_terms = lax.dot_general(

time: 468 us -> 425 us (0.908)
  waiting for transfers between devices: 316 us -> 265 us
  local copies, waits for them, and re-layouts: 18.7 us -> 24.1 us
    psum x1 -> x0, waiting for transfers between devices: 134 us -> none  [local(): prediction = lax.psum(partial_pred, ('row', 'col'))]
    all_gather x0 -> x1, waiting for transfers between devices: none -> 57.1 us  [local(): prediction = jnp.sum(lax.all_gather(partial_pred, ('row', 'col')), axis=0)]
    psum x1, waiting for transfers between devices: 112 us -> 139 us  [local(): lax.psum((select_rows(batch_index), select_rows(nystrom_index)), ('row',...]
    unnamed x21 -> x20, local copies, waits for them, and re-layouts: 3.47 us -> 8.94 us
  transfers between devices with their start and end apart: 4 -> 4, of which waited for: 3 -> 3; matrix products, arithmetic and copies ran while one was open for 11% -> 8% of each run, Pallas kernels for 0% -> 0%
where the time goes in v1:
time: 425 us; the launch traced here: 424 us
  waiting for transfers between devices  265 us (62%)
  matrix products  97.3 us (23%)
  local copies, waits for them, and re-layouts  24.1 us (6%)
  between operations  14 us (3%)
  blocking collectives  11.9 us (3%)
  other arithmetic  11.7 us (3%)
    psum x1, waiting for transfers between devices, local(): lax.psum((select_rows(batch_index), select_rows(nystrom_index)), ('row',...  139 us
    psum x1, waiting for transfers between devices, local(): correction = lax.psum(product(eigvecs, coeff), 'col')  69 us
    all_gather x1, waiting for transfers between devices, local(): prediction = jnp.sum(lax.all_gather(partial_pred, ('row', 'col')), axis=0)  57.1 us
    dot_general x4, matrix products, product(): jnp.dot(left, right, precision=lax.Precision.HIGHEST, preferred_element_t...  52 us
    dot_general x3, matrix products, kernel(): jnp.dot(left, right.T, precision=lax.Precision.HIGHEST, preferred_element...  38.3 us
    gather x2, local copies, waits for them, and re-layouts, select_rows(): fetched = jnp.take(centres, jnp.clip(local_rows, 0, rows_dev - 1), axis=0)  15.1 us
    psum x1, blocking collectives, local(): coeff = mode_scale[:, None] * lax.psum(mode_terms, 'row')  11.9 us
    unnamed x20, local copies, waits for them, and re-layouts  8.94 us
  transfers between devices with their start and end apart: 4, of which 3 were waited for; matrix products, arithmetic and copies ran while one was open for 8% of the time, Pallas kernels for 0%

profile of v1, /device:TPU:0, one launch (start us, length us, event | category | flops | bytes accessed | tf_op | source)
XLA Modules:
  0.0 424.2 jit_solution(8123085342271958507)
XLA Ops:
  7.2 0.0 copy-start
  7.2 0.0 all-reduce.6.cloned.1.call-start
  7.2 0.8 compare_and_fusion.1
  8.0 0.7 fusion.30
  8.8 0.7 compare_and_fusion.2
  9.5 1.4 copy.9
  10.8 1.0 gather_fusion
  11.9 14.1 %gather_fusion.1 = f32[4096,64]{1,0:T(8,128)} fusion(f32[2048,64]{1,0:T(8,128)S(1)} %copy.9, s32[4096]{0:T(1024)S(1)} %fusion.30), kind=kCustom, calls=%fused_computation.1 | custom fusion | bytes 2113536 | tf_op jit(solution)/shard_map/jit(_take)/gather | solution.py:32
  26.0 0.9 select_select_fusion.1
  26.9 6.0 %select_select_fusion = f32[4096,64]{1,0:T(8,128)} fusion(f32[4096,64]{1,0:T(8,128)} %gather_fusion.1, pred[4096]{0:T(1024)(128)(4,1)S(1)} %get-tuple-element.7, pred[4096]{0:T(1024)(128)(4,1)S(1)} %get-tuple-element.6), kind=kLoop, calls=%fused_computation.28 | loop fusion | flops 524288 | bytes 2105344 | tf_op jit(solution)/shard_map/jit(_where)/select_n | solution.py:33
  32.8 0.0 all-reduce.6.cloned.1.call-update
  32.9 0.0 all-gather.6.cloned.1.call-start
  32.9 0.0 copy-done.3
  32.9 0.1 multiply_reduce_fusion.2
  33.0 138.5 %all-reduce.6.cloned.1.call-done = (f32[512,64]{1,0:T(8,128)}, f32[4096,64]{1,0:T(8,128)}) async-done(((f32[512,64]{1,0:T(8,128)}, f32[4096,64]{1,0:T(8,128)}), (f32[512,64]{1,0:T(8,128)}, f32[4096,64]{1,0:T(8,128)})) %all-reduce.6.cloned.1.call-update) | async-done | bytes 1179664 | tf_op jit(solution)/shard_map/psum | solution.py:35
  171.5 1.1 multiply_reduce_fusion.3
  172.6 0.0 copy-start.2
  172.6 5.2 %fusion.13 = f32[2048,512]{0,1:T(8,128)S(1)} fusion(f32[512,64]{1,0:T(8,128)} %get-tuple-element.2, f32[2048,64]{0,1:T(8,128)S(1)} %copy-done.3, f32[512]{0:T(512)S(1)} %multiply_reduce_fusion.3, f32[2048]{0:T(1024)S(1)} %multiply_reduce_fusion.2), kind=kOutput, calls=%fused_computation.17 | convolution fusion | flops 810549248 | bytes 4859904 | tf_op jit(solution)/shard_map/dot_general | solution.py:12
  177.8 0.0 copy-start.1
  177.8 2.0 copy-done.1
  179.8 5.9 %fusion.36 = f32[512,64]{0,1:T(8,128)} fusion(f32[2048,512]{0,1:T(8,128)S(1)} %fusion.13, f32[2048,64]{0,1:T(8,128)} %param.8), kind=kOutput, calls=%fused_computation.56 | convolution fusion | flops 805306368 | bytes 4849664 | tf_op jit(solution)/shard_map/dot_general | solution.py:40
  185.7 0.0 all-gather.6.cloned.1.call-update
  185.8 0.2 all-reduce.4.cloned.1.call-start
  186.0 0.0 copy-done.2
  186.0 0.2 multiply_reduce_fusion.1
  186.2 0.0 copy-done.5
  186.2 3.1 fusion.26
  189.4 57.1 %all-gather.6.cloned.1.call-done = f32[16384,64]{0,1:T(8,128)} async-done(((f32[512,64]{0,1:T(8,128)}), f32[16384,64]{0,1:T(8,128)}) %all-gather.6.cloned.1.call-update) | async-done | bytes 4194320 | tf_op jit(solution)/shard_map/all_gather | solution.py:47
  246.5 4.6 %copy.11 = f32[8,8,32,512]{3,2,1,0:T(8,128)S(1)} copy(f32[8,8,32,512]{3,1,2,0:T(8,128)} %bitcast.40) | data formatting | bytes 8388608
  251.1 0.0 copy-start.7
  251.1 0.0 copy-start.8
  251.1 0.7 bitcast_reduce_fusion
  251.8 0.2 copy-done.7
  252.0 0.7 copy-done.4
  252.7 2.1 fusion.15
  254.8 0.0 copy-done
  254.8 1.0 convolution_bitcast_fusion.1
  255.8 11.9 %psum.30 = f32[128,64]{1,0:T(8,128)S(1)} all-reduce(f32[128,64]{1,0:T(8,128)S(1)} %convolution_bitcast_fusion.1), channel_id=1, replica_groups=mesh['row'=4,'col'=8] {'row'}, use_global_device_ids=true, to_apply=%region_7.8 | all-reduce | flops 8192 | bytes 65536 | tf_op jit(solution)/shard_map/psum | solution.py:57
  267.7 1.5 convolution_bitcast_fusion
  269.2 0.0 all-reduce.4.cloned.1.call-update
  269.2 0.3 all-gather.4.cloned.1.call-start
  269.5 0.6 multiply_reduce_fusion
  270.1 69.0 %all-reduce.4.cloned.1.call-done = f32[1024,64]{0,1:T(8,128)} async-done(((f32[1024,64]{0,1:T(8,128)}), f32[1024,64]{0,1:T(8,128)}) %all-reduce.4.cloned.1.call-update) | async-done | bytes 262160 | tf_op jit(solution)/shard_map/psum | solution.py:58
  339.0 0.0 all-gather.4.cloned.1.call-update
  339.1 30.1 %fusion.37 = f32[4096,2048]{0,1:T(8,128)} fusion(f32[4096,64]{1,0:T(8,128)S(1)} %copy-done.2, f32[2048,64]{0,1:T(8,128)S(1)} %copy-done.3), kind=kOutput, calls=%fused_computation.57 | convolution fusion | flops 6442450944 | bytes 35127296 | tf_op jit(solution)/shard_map/dot_general | solution.py:12
  369.1 42.7 %fusion.3 = f32[2048,64]{0,1:T(8,128)S(1)} fusion(f32[4096,64]{0,1:T(8,128)} %all-gather.4.cloned.1.call-done, f32[4096,2048]{0,1:T(8,128)} %fusion.37, f32[4096]{0:T(1024)S(1)} %multiply_reduce_fusion, f32[2048]{0:T(1024)S(1)} %multiply_reduce_fusion.2), kind=kOutput, calls=%fused_computation.6 | convolution fusion | flops 6484393984 | bytes 35151872 | tf_op jit(solution)/shard_map/dot_general | solution.py:21
  411.9 0.0 copy-done.6
  411.9 5.8 %fusion.14 = f32[2048,64]{0,1:T(8,128)} fusion(f32[2048,64]{0,1:T(8,128)S(1)} %fusion.3, f32[2048,512]{0,1:T(8,128)} %copy-done.1, f32[512,64]{0,1:T(8,128)S(1)} %sub.30), kind=kOutput, calls=%fused_computation.19 | convolution fusion | flops 805568512 | bytes 5373952 | tf_op jit(solution)/shard_map/dot_general | solution.py:21
  (8 shorter events, 0.0 us)
Async XLA Ops:
  7.2 247.6 %copy-start = (f32[1024,128]{1,0:T(8,128)S(1)}, f32[1024,128]{1,0:T(8,128)}, u32[]{:S(2)}) copy-start(f32[1024,128]{1,0:T(8,128)} %param.12) | copy-start | bytes 1572868
  7.2 164.4 %all-reduce.6.cloned.1.call-start = ((), (), s32[]{:S(2)}) async-start(), calls=%async_computation.3 | async-start | bytes 4718592 | tf_op jit(solution)/shard_map/psum | solution.py:35
  26.0 6.9 %copy-start.3 = (f32[2048,64]{0,1:T(8,128)S(1)}, f32[2048,64]{0,1:T(8,128)}, u32[]{:S(2)}) copy-start(f32[2048,64]{0,1:T(8,128)} %param.7) | copy-start | bytes 1572868
  32.9 213.6 %all-gather.6.cloned.1.call-start = ((), (), s32[]{:S(2)}) async-start(), calls=%async_computation.2 | async-start | bytes 4325376 | tf_op jit(solution)/shard_map/all_gather | solution.py:47
  172.6 13.4 %copy-start.2 = (f32[4096,64]{1,0:T(8,128)S(1)}, f32[4096,64]{1,0:T(8,128)}, u32[]{:S(2)}) copy-start(f32[4096,64]{1,0:T(8,128)} %get-tuple-element.3) | copy-start | bytes 3145732
  177.8 2.0 copy-start.1
  179.8 6.4 %copy-start.5 = (f32[512,64]{1,0:T(8,128)S(1)}, f32[512,64]{1,0:T(8,128)}, u32[]{:S(2)}) copy-start(f32[512,64]{1,0:T(8,128)} %get-tuple-element.2) | copy-start | bytes 393220
  185.8 153.3 %all-reduce.4.cloned.1.call-start = ((), (), s32[]{:S(2)}) async-start(), calls=%async_computation | async-start | bytes 524288 | tf_op jit(solution)/shard_map/psum | solution.py:58
  251.1 0.9 copy-start.7
  251.1 1.7 copy-start.4
  251.1 16.6 %copy-start.8 = (f32[128]{0:T(128)S(1)}, f32[128]{0:T(128)}, u32[]{:S(2)}) copy-start(f32[128]{0:T(128)} %param.13) | copy-start | bytes 1540
  252.7 159.1 %copy-start.6 = (f32[512,64]{0,1:T(8,128)}, f32[512,64]{0,1:T(8,128)S(1)}, u32[]{:S(2)}) copy-start(f32[512,64]{0,1:T(8,128)S(1)} %sub.30) | copy-start | bytes 393220
  269.2 99.9 %all-gather.4.cloned.1.call-start = ((), (), s32[]{:S(2)}) async-start(), calls=%async_computation.1 | async-start | bytes 1310720 | tf_op jit(solution)/shard_map/all_gather | solution.py:61
Sparse Core Ops, SparseCore 0:
  33.0 138.4 all-reduce.5
  185.9 60.5 all-gather.5
  269.3 69.6 all-reduce.3
  340.5 15.8 all-gather.3
